TPU v7x, 32 devices: a whole 2x2x4 slice. The times are simulated.
32 devices in a mesh: section: 4 (over x, core), obs: 8 (over z, y).
Axes of the slice: x: 2, y: 2, z: 4, core: 2. Of those that a mesh axis runs over, the one named last changes fastest.
Arguments:
- predictors: bfloat16 [4, 4, 20, 32768], P('section', None, None, 'obs'), may hold values from -5 to 5
- departures: float32 [4, 4, 32768], P('section', None, 'obs'), may hold values from -30 to 30
- obs_precision: float32 [4, 4, 32768], P('section', None, 'obs'), may hold values from 0.3 to 3
- qc_pass: int32 [4, 4, 32768], P('section', None, 'obs'), may hold values 0 or 1
- block_channel: int32 [4, 4, 256], P('section', None, 'obs'), may hold values from 0 to 2047, as said below
- stream_order: int32 [4], replicated, may hold values from 0 to 3, each once
- prior_coeffs: float32 [4, 20, 2048], P(None, None, 'obs'), may hold values from -1 to 1
- prior_info: float32 [4, 210, 2048], P(None, None, 'obs'), may hold values from -1 to 32, as said below
- memory_factor: float32 [2048], P('obs'), may hold values from 0.5 to 0.98
Outputs:
- coeffs: float32 [4, 4, 20, 2048], P('section', None, None, 'obs')
- information: float32 [4, 4, 210, 2048], P('section', None, None, 'obs')
Inputs may be any that keep to these rules, and one draw needn't show every extreme that they name: `block_channel`: among the 32 row blocks of one index of obs, at most 8 have channels in any one range of the 256 channels from a multiple of 256; in every window and stream one such range holds exactly 8 blocks of every index of obs. `stream_order`: each stream appears once. `prior_info`: for every stream and channel the 210 entries are the upper triangle, row by row, of a symmetric positive definite matrix of order 20.
All inputs are finite; a program needn't handle non-finite values. No bound on the sum of `qc_pass` on one device may be relied on, other than what follows from the above.
Results may differ from a plain program's by a relative error of at most 0.0038.
Values sent between devices are 32-bit elements; how exact they have to be, the bound alone decides.
A program may use at most 64 MiB of HBM per device.

v0:
```python
import jax
import jax.numpy as jnp
import numpy as np
from jax import lax
from jax.sharding import PartitionSpec as P

HUBER_SQ = 9.0
PRIOR_WEIGHT = 64.0


def from_behind(array, axis, by):
    size = lax.axis_size(axis)
    pairs = [(i, i + by) for i in range(size) if 0 <= i + by < size]
    return lax.ppermute(array, axis, pairs)


def upper_positions(dimension):
    return np.array(
        [i * dimension + j for i in range(dimension) for j in range(i, dimension)], dtype=np.int32
    )


def solve_packed(packed, target):
    dimension = target.shape[0]
    placing = {}
    counter = 0
    for i in range(dimension):
        for j in range(i, dimension):
            placing[i, j] = counter
            counter += 1
    factor = [[None] * dimension for i in range(dimension)]
    for j in range(dimension):
        pivot_root = jnp.sqrt(
            packed[placing[j, j]] - sum((factor[j][k] * factor[j][k] for k in range(j)))
        )
        factor[j][j] = pivot_root
        for i in range(j + 1, dimension):
            factor[i][j] = (
                packed[placing[j, i]] - sum((factor[i][k] * factor[j][k] for k in range(j)))
            ) / pivot_root
    forward = []
    for i in range(dimension):
        forward.append(
            (target[i] - sum((factor[i][k] * forward[k] for k in range(i)))) / factor[i][i]
        )
    backward = [None] * dimension
    for i in reversed(range(dimension)):
        backward[i] = (
            forward[i] - sum((factor[k][i] * backward[k] for k in range(i + 1, dimension)))
        ) / factor[i][i]
    return jnp.stack(backward)


def block_terms(predicted, departed, precision, passed, block_coeffs):
    pred_count, row_count = predicted.shape
    block_count = block_coeffs.shape[1]
    block_width = row_count // block_count
    upper_index = upper_positions(pred_count)
    shaped = predicted.reshape(pred_count, block_count, block_width)
    offset = jnp.sum(shaped.astype(jnp.float32) * block_coeffs[:, :, None], axis=0)
    residual = departed.reshape(block_count, block_width) - offset
    scale_row = precision.reshape(block_count, block_width)
    weight = (
        passed.reshape(block_count, block_width).astype(jnp.float32)
        * scale_row
        / (1.0 + scale_row * residual * residual / HUBER_SQ)
    )
    weighted = (weight[None] * shaped.astype(jnp.float32)).astype(jnp.bfloat16)
    chi_square = jnp.sum(weight * residual * residual)
    passed_count = jnp.sum(passed.astype(jnp.float32))
    gram_full = lax.dot_general(
        weighted, shaped, (((2,), (2,)), ((1,), (1,))), preferred_element_type=jnp.float32
    )
    gram_upper = gram_full.reshape(block_count, pred_count * pred_count)[:, upper_index]
    gradient = jnp.sum(weighted.astype(jnp.float32) * residual[None], axis=2).T
    return (jnp.concatenate([gram_upper, gradient], axis=1), jnp.stack([chi_square, passed_count]))


def local(
    predictors,
    departures,
    obs_precision,
    qc_pass,
    block_channel,
    stream_order,
    prior_coeffs,
    prior_info,
    memory_factor,
):
    section_count = lax.axis_size("section")
    obs_devices = lax.axis_size("obs")
    section_place = lax.axis_index("section")
    stream_count = stream_order.shape[0]
    local_channels = memory_factor.shape[0]
    block_count = block_channel.shape[2]
    pred_count = prior_coeffs.shape[1]
    tri_count = prior_info.shape[1]
    column_count = tri_count + pred_count
    capacity = 2 * block_count // obs_devices
    local_line = jnp.arange(local_channels, dtype=jnp.float32)
    owner_line = jnp.arange(obs_devices, dtype=jnp.int32)
    slot_line = jnp.arange(obs_devices * capacity, dtype=jnp.int32)
    highest = lax.Precision.HIGHEST

    def pack_blocks(block_sums, channel):
        owner_index = channel // local_channels
        inner_channel = channel % local_channels
        owner_hot = (owner_index[:, None] == owner_line[None, :]).astype(jnp.int32)
        ranking = jnp.sum((jnp.cumsum(owner_hot, axis=0) - 1) * owner_hot, axis=1)
        slot_of = owner_index * capacity + ranking
        placing = (slot_of[:, None] == slot_line[None, :]).astype(jnp.float32)
        send_rows = lax.dot_general(
            placing,
            block_sums,
            (((0,), (0,)), ((), ())),
            precision=highest,
            preferred_element_type=jnp.float32,
        ).reshape(obs_devices, capacity, column_count)
        send_channel = (
            lax.dot_general(
                placing,
                (inner_channel + 1).astype(jnp.float32),
                (((0,), (0,)), ((), ())),
                precision=highest,
                preferred_element_type=jnp.float32,
            ).reshape(obs_devices, capacity)
            - 1.0
        )
        return (send_rows, send_channel)

    def unpack_blocks(got_rows, got_channel):
        gather_hot = (got_channel.reshape(-1)[:, None] == local_line[None, :]).astype(jnp.float32)
        return lax.dot_general(
            got_rows.reshape(-1, column_count),
            gather_hot,
            (((0,), (0,)), ((), ())),
            precision=highest,
            preferred_element_type=jnp.float32,
        )

    def window_work(state_now, streams):
        beta_prior = state_now[:, :pred_count]
        info_prior = state_now[:, pred_count:]
        all_coeffs = lax.all_gather(beta_prior, "obs", axis=2, tiled=True)
        channel = jnp.take(block_channel[0], streams, axis=0)
        block_coeffs = jax.vmap(lambda coeff_rows, chan: jnp.take(coeff_rows, chan, axis=1))(
            all_coeffs, channel
        )
        block_sums, statistics = jax.vmap(block_terms)(
            jnp.take(predictors[0], streams, axis=0),
            jnp.take(departures[0], streams, axis=0),
            jnp.take(obs_precision[0], streams, axis=0),
            jnp.take(qc_pass[0], streams, axis=0),
            block_coeffs,
        )
        totals = lax.psum(statistics, "obs")
        send_rows, send_channel = jax.vmap(pack_blocks)(block_sums, channel)
        got_rows, got_channel = (
            lax.all_to_all(send_rows, "obs", split_axis=1, concat_axis=1, tiled=True),
            lax.all_to_all(send_channel, "obs", split_axis=1, concat_axis=1, tiled=True),
        )
        normal = jax.vmap(unpack_blocks)(got_rows, got_channel)
        inflation = (totals[:, 0] + PRIOR_WEIGHT) / (totals[:, 1] + PRIOR_WEIGHT)
        info_post = info_prior + normal[:, :tri_count] / inflation[:, None, None]
        beta_post = beta_prior + jax.vmap(solve_packed)(
            info_post, normal[:, tri_count:] / inflation[:, None, None]
        )
        outgoing = jnp.concatenate([beta_post, memory_factor[None, None, :] * info_post], axis=1)
        incoming = from_behind(outgoing, "section", 1)
        return (beta_post, info_post, incoming)

    def fresh_of(streams):
        return jnp.concatenate(
            [jnp.take(prior_coeffs, streams, axis=0), jnp.take(prior_info, streams, axis=0)], axis=1
        )

    coeff_start = jnp.zeros((1, stream_count, pred_count, local_channels), jnp.float32)
    info_start = jnp.zeros((1, stream_count, tri_count, local_channels), jnp.float32)

    def tick_step(t, loop_state):
        incoming, coeff_out, info_out = loop_state
        entry_index = t - section_place
        usable = (entry_index >= 0) & (entry_index < stream_count)
        slot_index = jnp.clip(entry_index, 0, stream_count - 1)
        streams = lax.dynamic_slice_in_dim(stream_order, slot_index, 1, 0)
        state_now = jnp.where(
            (section_place == 0) | jnp.logical_not(usable), fresh_of(streams), incoming
        )
        beta_post, info_post, incoming = window_work(state_now, streams)

        def store_entry(buffer, result):
            current = lax.dynamic_slice_in_dim(buffer, slot_index, 1, 1)
            updated = jnp.where(usable, result[None], current)
            return lax.dynamic_update_slice_in_dim(buffer, updated, slot_index, 1)

        return (incoming, store_entry(coeff_out, beta_post), store_entry(info_out, info_post))

    initial = (jnp.zeros((1, column_count, local_channels), jnp.float32), coeff_start, info_start)
    final_state = lax.fori_loop(0, stream_count + section_count - 1, tick_step, initial)
    return (final_state[1], final_state[2])


def solution(mesh):
    in_specs = (
        P("section", None, None, "obs"),
        P("section", None, "obs"),
        P("section", None, "obs"),
        P("section", None, "obs"),
        P("section", None, "obs"),
        P(),
        P(None, None, "obs"),
        P(None, None, "obs"),
        P("obs"),
    )
    out_specs = (P("section", None, None, "obs"), P("section", None, None, "obs"))
    return jax.shard_map(local, mesh=mesh, in_specs=in_specs, out_specs=out_specs, check_vma=False)
```

profile of v0, /device:TPU:1, one launch (start us, length us, event | category | flops | bytes accessed | tf_op | source)
XLA Modules:
  0.0 688.5 jit_solution(5905409147109336993)
XLA Ops:
  2.9 684.6 %while.38 = (s32[]{:T(128)}, f32[1,230,256]{2,1,0:T(8,128)S(1)}, f32[1,4,20,256]{3,1,2,0:T(4,128)S(1)}, f32[1,4,210,256]{3,1,2,0:T(4,128)S(1)}, s32[]{:T(128)}, ...) while((s32[]{:T(128)}, f32[1,230,256]{2,1,0:T(8,128)S(1)}, ...), condition=%wide.region_8.10_spmd.clone.clone, body=%wide.region_0.9_spmd.sunk.clone.clone.sunk | while | flops 57759508 | bytes 13853709 | solution.py:199
  7.5 6.4 all-to-all-start.1
  16.3 24.6 %all_gather.15 = f32[1,20,2048]{2,1,0:T(8,128)S(1)} all-gather(f32[1,20,256]{2,1,0:T(8,128)S(1)} %slice.5342), channel_id=1, replica_groups=mesh['section'=4,'obs'=8] {'obs'}, dimensions={2}, use_global_device_ids=true | all-gather | bytes 184320 | tf_op jit(solution)/shard_map/while/body/eval_jaxpr/all_gather | solution.py:144
  47.6 17.5 %psum.19 = f32[1,2]{1,0:T(1,128)S(1)} all-reduce(f32[1,2]{1,0:T(1,128)S(1)} %maximum_bitcast_fusion.6), channel_id=1, replica_groups=mesh['section'=4,'obs'=8] {'obs'}, use_global_device_ids=true, to_apply=%region_7.8 | all-reduce | flops 2 | bytes 16 | tf_op jit(solution)/shard_map/while/body/eval_jaxpr/psum | solution.py:156
  72.6 4.4 all-to-all-done
  83.2 15.7 %collective-permute-start = (f32[1,230,256]{2,1,0:T(8,128)S(1)}, f32[1,230,256]{2,1,0:T(8,128)S(1)}, u32[]{:S(2)}, u32[]{:S(2)}) collective-permute-start(f32[1,230,256]{2,1,0:T(8,128)S(1)} %pad_maximum_fusion.2), channel_id=1, source_target_pairs={{0,8},{8,16},{16,24},{1,9},{9,17},{17,25},{2,10},{10,18},{18,26},{... | collective-permute-start | bytes 706568 | tf_op jit(solution)/shard_map/while/body/eval_jaxpr/ppermute | solution.py:14
  99.3 5.9 dynamic_update_slice.31
  115.6 25.2 %all_gather.15 = f32[1,20,2048]{2,1,0:T(8,128)S(1)} all-gather(f32[1,20,256]{2,1,0:T(8,128)S(1)} %slice.5342), channel_id=1, replica_groups=mesh['section'=4,'obs'=8] {'obs'}, dimensions={2}, use_global_device_ids=true | all-gather | bytes 184320 | tf_op jit(solution)/shard_map/while/body/eval_jaxpr/all_gather | solution.py:144
  147.5 17.3 %psum.19 = f32[1,2]{1,0:T(1,128)S(1)} all-reduce(f32[1,2]{1,0:T(1,128)S(1)} %maximum_bitcast_fusion.6), channel_id=1, replica_groups=mesh['section'=4,'obs'=8] {'obs'}, use_global_device_ids=true, to_apply=%region_7.8 | all-reduce | flops 2 | bytes 16 | tf_op jit(solution)/shard_map/while/body/eval_jaxpr/psum | solution.py:156
  172.3 4.4 all-to-all-done
  182.9 13.1 %collective-permute-start = (f32[1,230,256]{2,1,0:T(8,128)S(1)}, f32[1,230,256]{2,1,0:T(8,128)S(1)}, u32[]{:S(2)}, u32[]{:S(2)}) collective-permute-start(f32[1,230,256]{2,1,0:T(8,128)S(1)} %pad_maximum_fusion.2), channel_id=1, source_target_pairs={{0,8},{8,16},{16,24},{1,9},{9,17},{17,25},{2,10},{10,18},{18,26},{... | collective-permute-start | bytes 706568 | tf_op jit(solution)/shard_map/while/body/eval_jaxpr/ppermute | solution.py:14
  196.4 5.9 dynamic_update_slice.31
  212.6 24.6 %all_gather.15 = f32[1,20,2048]{2,1,0:T(8,128)S(1)} all-gather(f32[1,20,256]{2,1,0:T(8,128)S(1)} %slice.5342), channel_id=1, replica_groups=mesh['section'=4,'obs'=8] {'obs'}, dimensions={2}, use_global_device_ids=true | all-gather | bytes 184320 | tf_op jit(solution)/shard_map/while/body/eval_jaxpr/all_gather | solution.py:144
  244.0 17.5 %psum.19 = f32[1,2]{1,0:T(1,128)S(1)} all-reduce(f32[1,2]{1,0:T(1,128)S(1)} %maximum_bitcast_fusion.6), channel_id=1, replica_groups=mesh['section'=4,'obs'=8] {'obs'}, use_global_device_ids=true, to_apply=%region_7.8 | all-reduce | flops 2 | bytes 16 | tf_op jit(solution)/shard_map/while/body/eval_jaxpr/psum | solution.py:156
  279.6 13.4 %collective-permute-start = (f32[1,230,256]{2,1,0:T(8,128)S(1)}, f32[1,230,256]{2,1,0:T(8,128)S(1)}, u32[]{:S(2)}, u32[]{:S(2)}) collective-permute-start(f32[1,230,256]{2,1,0:T(8,128)S(1)} %pad_maximum_fusion.2), channel_id=1, source_target_pairs={{0,8},{8,16},{16,24},{1,9},{9,17},{17,25},{2,10},{10,18},{18,26},{... | collective-permute-start | bytes 706568 | tf_op jit(solution)/shard_map/while/body/eval_jaxpr/ppermute | solution.py:14
  293.4 5.9 dynamic_update_slice.31
  309.7 24.8 %all_gather.15 = f32[1,20,2048]{2,1,0:T(8,128)S(1)} all-gather(f32[1,20,256]{2,1,0:T(8,128)S(1)} %slice.5342), channel_id=1, replica_groups=mesh['section'=4,'obs'=8] {'obs'}, dimensions={2}, use_global_device_ids=true | all-gather | bytes 184320 | tf_op jit(solution)/shard_map/while/body/eval_jaxpr/all_gather | solution.py:144
  341.3 17.6 %psum.19 = f32[1,2]{1,0:T(1,128)S(1)} all-reduce(f32[1,2]{1,0:T(1,128)S(1)} %maximum_bitcast_fusion.6), channel_id=1, replica_groups=mesh['section'=4,'obs'=8] {'obs'}, use_global_device_ids=true, to_apply=%region_7.8 | all-reduce | flops 2 | bytes 16 | tf_op jit(solution)/shard_map/while/body/eval_jaxpr/psum | solution.py:156
  377.0 13.1 %collective-permute-start = (f32[1,230,256]{2,1,0:T(8,128)S(1)}, f32[1,230,256]{2,1,0:T(8,128)S(1)}, u32[]{:S(2)}, u32[]{:S(2)}) collective-permute-start(f32[1,230,256]{2,1,0:T(8,128)S(1)} %pad_maximum_fusion.2), channel_id=1, source_target_pairs={{0,8},{8,16},{16,24},{1,9},{9,17},{17,25},{2,10},{10,18},{18,26},{... | collective-permute-start | bytes 706568 | tf_op jit(solution)/shard_map/while/body/eval_jaxpr/ppermute | solution.py:14
  390.5 5.9 dynamic_update_slice.31
  406.7 24.9 %all_gather.15 = f32[1,20,2048]{2,1,0:T(8,128)S(1)} all-gather(f32[1,20,256]{2,1,0:T(8,128)S(1)} %slice.5342), channel_id=1, replica_groups=mesh['section'=4,'obs'=8] {'obs'}, dimensions={2}, use_global_device_ids=true | all-gather | bytes 184320 | tf_op jit(solution)/shard_map/while/body/eval_jaxpr/all_gather | solution.py:144
  438.4 17.2 %psum.19 = f32[1,2]{1,0:T(1,128)S(1)} all-reduce(f32[1,2]{1,0:T(1,128)S(1)} %maximum_bitcast_fusion.6), channel_id=1, replica_groups=mesh['section'=4,'obs'=8] {'obs'}, use_global_device_ids=true, to_apply=%region_7.8 | all-reduce | flops 2 | bytes 16 | tf_op jit(solution)/shard_map/while/body/eval_jaxpr/psum | solution.py:156
  473.8 13.4 %collective-permute-start = (f32[1,230,256]{2,1,0:T(8,128)S(1)}, f32[1,230,256]{2,1,0:T(8,128)S(1)}, u32[]{:S(2)}, u32[]{:S(2)}) collective-permute-start(f32[1,230,256]{2,1,0:T(8,128)S(1)} %pad_maximum_fusion.2), channel_id=1, source_target_pairs={{0,8},{8,16},{16,24},{1,9},{9,17},{17,25},{2,10},{10,18},{18,26},{... | collective-permute-start | bytes 706568 | tf_op jit(solution)/shard_map/while/body/eval_jaxpr/ppermute | solution.py:14
  487.5 5.9 dynamic_update_slice.31
  503.8 24.8 %all_gather.15 = f32[1,20,2048]{2,1,0:T(8,128)S(1)} all-gather(f32[1,20,256]{2,1,0:T(8,128)S(1)} %slice.5342), channel_id=1, replica_groups=mesh['section'=4,'obs'=8] {'obs'}, dimensions={2}, use_global_device_ids=true | all-gather | bytes 184320 | tf_op jit(solution)/shard_map/while/body/eval_jaxpr/all_gather | solution.py:144
  535.4 17.5 %psum.19 = f32[1,2]{1,0:T(1,128)S(1)} all-reduce(f32[1,2]{1,0:T(1,128)S(1)} %maximum_bitcast_fusion.6), channel_id=1, replica_groups=mesh['section'=4,'obs'=8] {'obs'}, use_global_device_ids=true, to_apply=%region_7.8 | all-reduce | flops 2 | bytes 16 | tf_op jit(solution)/shard_map/while/body/eval_jaxpr/psum | solution.py:156
  571.0 13.2 %collective-permute-start = (f32[1,230,256]{2,1,0:T(8,128)S(1)}, f32[1,230,256]{2,1,0:T(8,128)S(1)}, u32[]{:S(2)}, u32[]{:S(2)}) collective-permute-start(f32[1,230,256]{2,1,0:T(8,128)S(1)} %pad_maximum_fusion.2), channel_id=1, source_target_pairs={{0,8},{8,16},{16,24},{1,9},{9,17},{17,25},{2,10},{10,18},{18,26},{... | collective-permute-start | bytes 706568 | tf_op jit(solution)/shard_map/while/body/eval_jaxpr/ppermute | solution.py:14
  584.6 5.9 dynamic_update_slice.31
  600.9 24.5 %all_gather.15 = f32[1,20,2048]{2,1,0:T(8,128)S(1)} all-gather(f32[1,20,256]{2,1,0:T(8,128)S(1)} %slice.5342), channel_id=1, replica_groups=mesh['section'=4,'obs'=8] {'obs'}, dimensions={2}, use_global_device_ids=true | all-gather | bytes 184320 | tf_op jit(solution)/shard_map/while/body/eval_jaxpr/all_gather | solution.py:144
  632.1 18.0 %psum.19 = f32[1,2]{1,0:T(1,128)S(1)} all-reduce(f32[1,2]{1,0:T(1,128)S(1)} %maximum_bitcast_fusion.6), channel_id=1, replica_groups=mesh['section'=4,'obs'=8] {'obs'}, use_global_device_ids=true, to_apply=%region_7.8 | all-reduce | flops 2 | bytes 16 | tf_op jit(solution)/shard_map/while/body/eval_jaxpr/psum | solution.py:156
  668.2 13.1 %collective-permute-start = (f32[1,230,256]{2,1,0:T(8,128)S(1)}, f32[1,230,256]{2,1,0:T(8,128)S(1)}, u32[]{:S(2)}, u32[]{:S(2)}) collective-permute-start(f32[1,230,256]{2,1,0:T(8,128)S(1)} %pad_maximum_fusion.2), channel_id=1, source_target_pairs={{0,8},{8,16},{16,24},{1,9},{9,17},{17,25},{2,10},{10,18},{18,26},{... | collective-permute-start | bytes 706568 | tf_op jit(solution)/shard_map/while/body/eval_jaxpr/ppermute | solution.py:14
  681.7 5.9 dynamic_update_slice.31
  (648 shorter events, 214.5 us)
Async XLA Ops:
  2.2 0.7 copy-start.4
  2.3 0.7 copy-start.5
  7.5 60.4 %all-to-all-start.1 = ((f32[1,8,8]{2,0,1:T(1,128)}), f32[1,8,8]{2,0,1:T(1,128)S(1)}, u32[]{:S(2)}, u32[]{:S(2)}) async-start(f32[1,8,8]{2,0,1:T(1,128)} %bitcast.2454), calls=%async_computation.1 | async-start | bytes 8192 | tf_op jit(solution)/shard_map/while/body/eval_jaxpr/all_to_all | solution.py:160
  68.0 9.1 %all-to-all-start = ((f32[1,8,8,230]{3,2,0,1:T(8,128)}), f32[1,8,8,230]{3,2,0,1:T(8,128)S(1)}, u32[]{:S(2)}, u32[]{:S(2)}) async-start(f32[1,8,8,230]{3,2,0,1:T(8,128)} %convolution_bitcast_fusion.4), calls=%async_computation | async-start | bytes 131072 | tf_op jit(solution)/shard_map/while/body/eval_jaxpr/all_to_all | solution.py:159
  80.7 0.7 copy-start.1
  83.2 22.0 %collective-permute-start = (f32[1,230,256]{2,1,0:T(8,128)S(1)}, f32[1,230,256]{2,1,0:T(8,128)S(1)}, u32[]{:S(2)}, u32[]{:S(2)}) collective-permute-start(f32[1,230,256]{2,1,0:T(8,128)S(1)} %pad_maximum_fusion.2), channel_id=1, source_target_pairs={{0,8},{8,16},{16,24},{1,9},{9,17},{17,25},{2,10},{10,18},{18,26},{... | collective-permute-start | bytes 706568 | tf_op jit(solution)/shard_map/while/body/eval_jaxpr/ppermute | solution.py:14
  109.8 57.8 %all-to-all-start.1 = ((f32[1,8,8]{2,0,1:T(1,128)}), f32[1,8,8]{2,0,1:T(1,128)S(1)}, u32[]{:S(2)}, u32[]{:S(2)}) async-start(f32[1,8,8]{2,0,1:T(1,128)} %bitcast.2454), calls=%async_computation.1 | async-start | bytes 8192 | tf_op jit(solution)/shard_map/while/body/eval_jaxpr/all_to_all | solution.py:160
  167.6 9.1 %all-to-all-start = ((f32[1,8,8,230]{3,2,0,1:T(8,128)}), f32[1,8,8,230]{3,2,0,1:T(8,128)S(1)}, u32[]{:S(2)}, u32[]{:S(2)}) async-start(f32[1,8,8,230]{3,2,0,1:T(8,128)} %convolution_bitcast_fusion.4), calls=%async_computation | async-start | bytes 131072 | tf_op jit(solution)/shard_map/while/body/eval_jaxpr/all_to_all | solution.py:159
  180.4 0.7 copy-start.1
  182.9 19.4 %collective-permute-start = (f32[1,230,256]{2,1,0:T(8,128)S(1)}, f32[1,230,256]{2,1,0:T(8,128)S(1)}, u32[]{:S(2)}, u32[]{:S(2)}) collective-permute-start(f32[1,230,256]{2,1,0:T(8,128)S(1)} %pad_maximum_fusion.2), channel_id=1, source_target_pairs={{0,8},{8,16},{16,24},{1,9},{9,17},{17,25},{2,10},{10,18},{18,26},{... | collective-permute-start | bytes 706568 | tf_op jit(solution)/shard_map/while/body/eval_jaxpr/ppermute | solution.py:14
  206.9 57.5 %all-to-all-start.1 = ((f32[1,8,8]{2,0,1:T(1,128)}), f32[1,8,8]{2,0,1:T(1,128)S(1)}, u32[]{:S(2)}, u32[]{:S(2)}) async-start(f32[1,8,8]{2,0,1:T(1,128)} %bitcast.2454), calls=%async_computation.1 | async-start | bytes 8192 | tf_op jit(solution)/shard_map/while/body/eval_jaxpr/all_to_all | solution.py:160
  264.4 9.1 %all-to-all-start = ((f32[1,8,8,230]{3,2,0,1:T(8,128)}), f32[1,8,8,230]{3,2,0,1:T(8,128)S(1)}, u32[]{:S(2)}, u32[]{:S(2)}) async-start(f32[1,8,8,230]{3,2,0,1:T(8,128)} %convolution_bitcast_fusion.4), calls=%async_computation | async-start | bytes 131072 | tf_op jit(solution)/shard_map/while/body/eval_jaxpr/all_to_all | solution.py:159
  277.1 0.7 copy-start.1
  279.6 19.7 %collective-permute-start = (f32[1,230,256]{2,1,0:T(8,128)S(1)}, f32[1,230,256]{2,1,0:T(8,128)S(1)}, u32[]{:S(2)}, u32[]{:S(2)}) collective-permute-start(f32[1,230,256]{2,1,0:T(8,128)S(1)} %pad_maximum_fusion.2), channel_id=1, source_target_pairs={{0,8},{8,16},{16,24},{1,9},{9,17},{17,25},{2,10},{10,18},{18,26},{... | collective-permute-start | bytes 706568 | tf_op jit(solution)/shard_map/while/body/eval_jaxpr/ppermute | solution.py:14
  303.9 57.8 %all-to-all-start.1 = ((f32[1,8,8]{2,0,1:T(1,128)}), f32[1,8,8]{2,0,1:T(1,128)S(1)}, u32[]{:S(2)}, u32[]{:S(2)}) async-start(f32[1,8,8]{2,0,1:T(1,128)} %bitcast.2454), calls=%async_computation.1 | async-start | bytes 8192 | tf_op jit(solution)/shard_map/while/body/eval_jaxpr/all_to_all | solution.py:160
  361.8 9.1 %all-to-all-start = ((f32[1,8,8,230]{3,2,0,1:T(8,128)}), f32[1,8,8,230]{3,2,0,1:T(8,128)S(1)}, u32[]{:S(2)}, u32[]{:S(2)}) async-start(f32[1,8,8,230]{3,2,0,1:T(8,128)} %convolution_bitcast_fusion.4), calls=%async_computation | async-start | bytes 131072 | tf_op jit(solution)/shard_map/while/body/eval_jaxpr/all_to_all | solution.py:159
  374.5 0.7 copy-start.1
  377.0 19.4 %collective-permute-start = (f32[1,230,256]{2,1,0:T(8,128)S(1)}, f32[1,230,256]{2,1,0:T(8,128)S(1)}, u32[]{:S(2)}, u32[]{:S(2)}) collective-permute-start(f32[1,230,256]{2,1,0:T(8,128)S(1)} %pad_maximum_fusion.2), channel_id=1, source_target_pairs={{0,8},{8,16},{16,24},{1,9},{9,17},{17,25},{2,10},{10,18},{18,26},{... | collective-permute-start | bytes 706568 | tf_op jit(solution)/shard_map/while/body/eval_jaxpr/ppermute | solution.py:14
  401.0 57.5 %all-to-all-start.1 = ((f32[1,8,8]{2,0,1:T(1,128)}), f32[1,8,8]{2,0,1:T(1,128)S(1)}, u32[]{:S(2)}, u32[]{:S(2)}) async-start(f32[1,8,8]{2,0,1:T(1,128)} %bitcast.2454), calls=%async_computation.1 | async-start | bytes 8192 | tf_op jit(solution)/shard_map/while/body/eval_jaxpr/all_to_all | solution.py:160
  458.5 9.1 %all-to-all-start = ((f32[1,8,8,230]{3,2,0,1:T(8,128)}), f32[1,8,8,230]{3,2,0,1:T(8,128)S(1)}, u32[]{:S(2)}, u32[]{:S(2)}) async-start(f32[1,8,8,230]{3,2,0,1:T(8,128)} %convolution_bitcast_fusion.4), calls=%async_computation | async-start | bytes 131072 | tf_op jit(solution)/shard_map/while/body/eval_jaxpr/all_to_all | solution.py:159
  471.3 0.7 copy-start.1
  473.8 19.7 %collective-permute-start = (f32[1,230,256]{2,1,0:T(8,128)S(1)}, f32[1,230,256]{2,1,0:T(8,128)S(1)}, u32[]{:S(2)}, u32[]{:S(2)}) collective-permute-start(f32[1,230,256]{2,1,0:T(8,128)S(1)} %pad_maximum_fusion.2), channel_id=1, source_target_pairs={{0,8},{8,16},{16,24},{1,9},{9,17},{17,25},{2,10},{10,18},{18,26},{... | collective-permute-start | bytes 706568 | tf_op jit(solution)/shard_map/while/body/eval_jaxpr/ppermute | solution.py:14
  498.1 57.7 %all-to-all-start.1 = ((f32[1,8,8]{2,0,1:T(1,128)}), f32[1,8,8]{2,0,1:T(1,128)S(1)}, u32[]{:S(2)}, u32[]{:S(2)}) async-start(f32[1,8,8]{2,0,1:T(1,128)} %bitcast.2454), calls=%async_computation.1 | async-start | bytes 8192 | tf_op jit(solution)/shard_map/while/body/eval_jaxpr/all_to_all | solution.py:160
  555.8 9.1 %all-to-all-start = ((f32[1,8,8,230]{3,2,0,1:T(8,128)}), f32[1,8,8,230]{3,2,0,1:T(8,128)S(1)}, u32[]{:S(2)}, u32[]{:S(2)}) async-start(f32[1,8,8,230]{3,2,0,1:T(8,128)} %convolution_bitcast_fusion.4), calls=%async_computation | async-start | bytes 131072 | tf_op jit(solution)/shard_map/while/body/eval_jaxpr/all_to_all | solution.py:159
  568.5 0.7 copy-start.1
  571.0 19.5 %collective-permute-start = (f32[1,230,256]{2,1,0:T(8,128)S(1)}, f32[1,230,256]{2,1,0:T(8,128)S(1)}, u32[]{:S(2)}, u32[]{:S(2)}) collective-permute-start(f32[1,230,256]{2,1,0:T(8,128)S(1)} %pad_maximum_fusion.2), channel_id=1, source_target_pairs={{0,8},{8,16},{16,24},{1,9},{9,17},{17,25},{2,10},{10,18},{18,26},{... | collective-permute-start | bytes 706568 | tf_op jit(solution)/shard_map/while/body/eval_jaxpr/ppermute | solution.py:14
  595.1 57.8 %all-to-all-start.1 = ((f32[1,8,8]{2,0,1:T(1,128)}), f32[1,8,8]{2,0,1:T(1,128)S(1)}, u32[]{:S(2)}, u32[]{:S(2)}) async-start(f32[1,8,8]{2,0,1:T(1,128)} %bitcast.2454), calls=%async_computation.1 | async-start | bytes 8192 | tf_op jit(solution)/shard_map/while/body/eval_jaxpr/all_to_all | solution.py:160
  652.9 9.1 %all-to-all-start = ((f32[1,8,8,230]{3,2,0,1:T(8,128)}), f32[1,8,8,230]{3,2,0,1:T(8,128)S(1)}, u32[]{:S(2)}, u32[]{:S(2)}) async-start(f32[1,8,8,230]{3,2,0,1:T(8,128)} %convolution_bitcast_fusion.4), calls=%async_computation | async-start | bytes 131072 | tf_op jit(solution)/shard_map/while/body/eval_jaxpr/all_to_all | solution.py:159
  665.7 0.7 copy-start.1
  668.2 19.4 %collective-permute-start = (f32[1,230,256]{2,1,0:T(8,128)S(1)}, f32[1,230,256]{2,1,0:T(8,128)S(1)}, u32[]{:S(2)}, u32[]{:S(2)}) collective-permute-start(f32[1,230,256]{2,1,0:T(8,128)S(1)} %pad_maximum_fusion.2), channel_id=1, source_target_pairs={{0,8},{8,16},{16,24},{1,9},{9,17},{17,25},{2,10},{10,18},{18,26},{... | collective-permute-start | bytes 706568 | tf_op jit(solution)/shard_map/while/body/eval_jaxpr/ppermute | solution.py:14
  687.6 0.9 copy-start.2
  687.6 0.9 copy-start.3
  (15 other events, 9.7 us)
where the time goes:
time: 692 us; the launch traced here: 689 us
  blocking collectives  296 us (43%)
  starting transfers between devices  145 us (21%)
  local copies, waits for them, and re-layouts  109 us (16%)
  other arithmetic  68.2 us (10%)
  waiting for transfers between devices  30.8 us (4%)
  loops' own time  25.7 us (4%)
  matrix products  12.9 us (2%)
    all_gather x7, blocking collectives, window_work(): all_coeffs = lax.all_gather(beta_prior, 'obs', axis=2, tiled=True)  173 us
    psum x7, blocking collectives, window_work(): totals = lax.psum(statistics, 'obs')  123 us
    ppermute x7, starting transfers between devices, from_behind(): return lax.ppermute(array, axis, pairs)  95 us
    dynamic_update_slice x28, local copies, waits for them, and re-layouts, store_entry(): return lax.dynamic_update_slice_in_dim(buffer, updated, slot_index, 1)  43.8 us
    all_to_all x7, waiting for transfers between devices, window_work(): lax.all_to_all(send_rows, 'obs', split_axis=1, concat_axis=1, tiled=True)  30.8 us
    all_to_all x7, starting transfers between devices, window_work(): lax.all_to_all(send_channel, 'obs', split_axis=1, concat_axis=1, tiled=True)  26.2 us
    another operation x1, loops' own time, local(): lax.fori_loop(0, stream_count + section_count - 1, tick_step, initial)  25.7 us
    all_to_all x7, starting transfers between devices, window_work(): lax.all_to_all(send_rows, 'obs', split_axis=1, concat_axis=1, tiled=True)  23.5 us
  transfers between devices with their start and end apart: 21, of which 7 were waited for; matrix products, arithmetic and copies ran while one was open for 18% of the time, Pallas kernels for 0%

commit v1 on v0

--- a/solution.py
+++ b/solution.py
@@ -141,7 +141,7 @@
     def window_work(state_now, streams):
         beta_prior = state_now[:, :pred_count]
         info_prior = state_now[:, pred_count:]
-        all_coeffs = lax.all_gather(beta_prior, "obs", axis=2, tiled=True)
+        all_coeffs = jnp.concatenate(lax.all_gather(beta_prior, "obs"), axis=2)
         channel = jnp.take(block_channel[0], streams, axis=0)
         block_coeffs = jax.vmap(lambda coeff_rows, chan: jnp.take(coeff_rows, chan, axis=1))(
             all_coeffs, channel

time: 692 us -> 692 us (level)
  no operation moved by 1% of the time
where the time goes in v1:
time: 692 us; the launch traced here: 689 us
  blocking collectives  296 us (43%)
  starting transfers between devices  145 us (21%)
  local copies, waits for them, and re-layouts  109 us (16%)
  other arithmetic  68.2 us (10%)
  waiting for transfers between devices  30.8 us (4%)
  loops' own time  25.7 us (4%)
  matrix products  12.9 us (2%)
    all_gather x7, blocking collectives, window_work(): all_coeffs = jnp.concatenate(lax.all_gather(beta_prior, 'obs'), axis=2)  173 us
    psum x7, blocking collectives, window_work(): totals = lax.psum(statistics, 'obs')  123 us
    ppermute x7, starting transfers between devices, from_behind(): return lax.ppermute(array, axis, pairs)  95 us
    dynamic_update_slice x28, local copies, waits for them, and re-layouts, store_entry(): return lax.dynamic_update_slice_in_dim(buffer, updated, slot_index, 1)  43.8 us
    all_to_all x7, waiting for transfers between devices, window_work(): lax.all_to_all(send_rows, 'obs', split_axis=1, concat_axis=1, tiled=True)  30.8 us
    all_to_all x7, starting transfers between devices, window_work(): lax.all_to_all(send_channel, 'obs', split_axis=1, concat_axis=1, tiled=True)  26.2 us
    another operation x1, loops' own time, local(): lax.fori_loop(0, stream_count + section_count - 1, tick_step, initial)  25.7 us
    all_to_all x7, starting transfers between devices, window_work(): lax.all_to_all(send_rows, 'obs', split_axis=1, concat_axis=1, tiled=True)  23.5 us
  transfers between devices with their start and end apart: 21, of which 7 were waited for; matrix products, arithmetic and copies ran while one was open for 18% of the time, Pallas kernels for 0%

profile of v1, /device:TPU:1, one launch (start us, length us, event | category | flops | bytes accessed | tf_op | source)
XLA Modules:
  0.0 688.5 jit_solution(9051573476740157524)
XLA Ops:
  2.9 684.6 %while.38 = (s32[]{:T(128)}, f32[1,230,256]{2,1,0:T(8,128)S(1)}, f32[1,4,20,256]{3,1,2,0:T(4,128)S(1)}, f32[1,4,210,256]{3,1,2,0:T(4,128)S(1)}, s32[]{:T(128)}, ...) while((s32[]{:T(128)}, f32[1,230,256]{2,1,0:T(8,128)S(1)}, ...), condition=%wide.region_8.10_spmd.clone.clone, body=%wide.region_0.9_spmd.sunk.clone.clone.sunk | while | flops 57759508 | bytes 13853709 | solution.py:199
  7.5 6.4 all-to-all-start.1
  16.3 24.6 %all-gather.3 = f32[8,20,256]{2,1,0:T(8,128)S(1)} all-gather(f32[1,20,256]{2,1,0:T(8,128)S(1)} %slice.5342), channel_id=2, replica_groups=mesh['section'=4,'obs'=8] {'obs'}, dimensions={0}, use_global_device_ids=true | all-gather | bytes 184320 | tf_op jit(solution)/shard_map/while/body/eval_jaxpr/all_gather | solution.py:144
  47.6 17.5 %psum.19 = f32[1,2]{1,0:T(1,128)S(1)} all-reduce(f32[1,2]{1,0:T(1,128)S(1)} %maximum_bitcast_fusion.6), channel_id=1, replica_groups=mesh['section'=4,'obs'=8] {'obs'}, use_global_device_ids=true, to_apply=%region_7.8 | all-reduce | flops 2 | bytes 16 | tf_op jit(solution)/shard_map/while/body/eval_jaxpr/psum | solution.py:156
  72.6 4.4 all-to-all-done
  83.2 15.7 %collective-permute-start = (f32[1,230,256]{2,1,0:T(8,128)S(1)}, f32[1,230,256]{2,1,0:T(8,128)S(1)}, u32[]{:S(2)}, u32[]{:S(2)}) collective-permute-start(f32[1,230,256]{2,1,0:T(8,128)S(1)} %pad_maximum_fusion.2), channel_id=1, source_target_pairs={{0,8},{8,16},{16,24},{1,9},{9,17},{17,25},{2,10},{10,18},{18,26},{... | collective-permute-start | bytes 706568 | tf_op jit(solution)/shard_map/while/body/eval_jaxpr/ppermute | solution.py:14
  99.3 5.9 dynamic_update_slice.31
  115.6 25.2 %all-gather.3 = f32[8,20,256]{2,1,0:T(8,128)S(1)} all-gather(f32[1,20,256]{2,1,0:T(8,128)S(1)} %slice.5342), channel_id=2, replica_groups=mesh['section'=4,'obs'=8] {'obs'}, dimensions={0}, use_global_device_ids=true | all-gather | bytes 184320 | tf_op jit(solution)/shard_map/while/body/eval_jaxpr/all_gather | solution.py:144
  147.5 17.3 %psum.19 = f32[1,2]{1,0:T(1,128)S(1)} all-reduce(f32[1,2]{1,0:T(1,128)S(1)} %maximum_bitcast_fusion.6), channel_id=1, replica_groups=mesh['section'=4,'obs'=8] {'obs'}, use_global_device_ids=true, to_apply=%region_7.8 | all-reduce | flops 2 | bytes 16 | tf_op jit(solution)/shard_map/while/body/eval_jaxpr/psum | solution.py:156
  172.3 4.4 all-to-all-done
  182.9 13.1 %collective-permute-start = (f32[1,230,256]{2,1,0:T(8,128)S(1)}, f32[1,230,256]{2,1,0:T(8,128)S(1)}, u32[]{:S(2)}, u32[]{:S(2)}) collective-permute-start(f32[1,230,256]{2,1,0:T(8,128)S(1)} %pad_maximum_fusion.2), channel_id=1, source_target_pairs={{0,8},{8,16},{16,24},{1,9},{9,17},{17,25},{2,10},{10,18},{18,26},{... | collective-permute-start | bytes 706568 | tf_op jit(solution)/shard_map/while/body/eval_jaxpr/ppermute | solution.py:14
  196.4 5.9 dynamic_update_slice.31
  212.6 24.6 %all-gather.3 = f32[8,20,256]{2,1,0:T(8,128)S(1)} all-gather(f32[1,20,256]{2,1,0:T(8,128)S(1)} %slice.5342), channel_id=2, replica_groups=mesh['section'=4,'obs'=8] {'obs'}, dimensions={0}, use_global_device_ids=true | all-gather | bytes 184320 | tf_op jit(solution)/shard_map/while/body/eval_jaxpr/all_gather | solution.py:144
  244.0 17.5 %psum.19 = f32[1,2]{1,0:T(1,128)S(1)} all-reduce(f32[1,2]{1,0:T(1,128)S(1)} %maximum_bitcast_fusion.6), channel_id=1, replica_groups=mesh['section'=4,'obs'=8] {'obs'}, use_global_device_ids=true, to_apply=%region_7.8 | all-reduce | flops 2 | bytes 16 | tf_op jit(solution)/shard_map/while/body/eval_jaxpr/psum | solution.py:156
  279.6 13.4 %collective-permute-start = (f32[1,230,256]{2,1,0:T(8,128)S(1)}, f32[1,230,256]{2,1,0:T(8,128)S(1)}, u32[]{:S(2)}, u32[]{:S(2)}) collective-permute-start(f32[1,230,256]{2,1,0:T(8,128)S(1)} %pad_maximum_fusion.2), channel_id=1, source_target_pairs={{0,8},{8,16},{16,24},{1,9},{9,17},{17,25},{2,10},{10,18},{18,26},{... | collective-permute-start | bytes 706568 | tf_op jit(solution)/shard_map/while/body/eval_jaxpr/ppermute | solution.py:14
  293.4 5.9 dynamic_update_slice.31
  309.7 24.8 %all-gather.3 = f32[8,20,256]{2,1,0:T(8,128)S(1)} all-gather(f32[1,20,256]{2,1,0:T(8,128)S(1)} %slice.5342), channel_id=2, replica_groups=mesh['section'=4,'obs'=8] {'obs'}, dimensions={0}, use_global_device_ids=true | all-gather | bytes 184320 | tf_op jit(solution)/shard_map/while/body/eval_jaxpr/all_gather | solution.py:144
  341.3 17.6 %psum.19 = f32[1,2]{1,0:T(1,128)S(1)} all-reduce(f32[1,2]{1,0:T(1,128)S(1)} %maximum_bitcast_fusion.6), channel_id=1, replica_groups=mesh['section'=4,'obs'=8] {'obs'}, use_global_device_ids=true, to_apply=%region_7.8 | all-reduce | flops 2 | bytes 16 | tf_op jit(solution)/shard_map/while/body/eval_jaxpr/psum | solution.py:156
  377.0 13.1 %collective-permute-start = (f32[1,230,256]{2,1,0:T(8,128)S(1)}, f32[1,230,256]{2,1,0:T(8,128)S(1)}, u32[]{:S(2)}, u32[]{:S(2)}) collective-permute-start(f32[1,230,256]{2,1,0:T(8,128)S(1)} %pad_maximum_fusion.2), channel_id=1, source_target_pairs={{0,8},{8,16},{16,24},{1,9},{9,17},{17,25},{2,10},{10,18},{18,26},{... | collective-permute-start | bytes 706568 | tf_op jit(solution)/shard_map/while/body/eval_jaxpr/ppermute | solution.py:14
  390.5 5.9 dynamic_update_slice.31
  406.7 24.9 %all-gather.3 = f32[8,20,256]{2,1,0:T(8,128)S(1)} all-gather(f32[1,20,256]{2,1,0:T(8,128)S(1)} %slice.5342), channel_id=2, replica_groups=mesh['section'=4,'obs'=8] {'obs'}, dimensions={0}, use_global_device_ids=true | all-gather | bytes 184320 | tf_op jit(solution)/shard_map/while/body/eval_jaxpr/all_gather | solution.py:144
  438.4 17.2 %psum.19 = f32[1,2]{1,0:T(1,128)S(1)} all-reduce(f32[1,2]{1,0:T(1,128)S(1)} %maximum_bitcast_fusion.6), channel_id=1, replica_groups=mesh['section'=4,'obs'=8] {'obs'}, use_global_device_ids=true, to_apply=%region_7.8 | all-reduce | flops 2 | bytes 16 | tf_op jit(solution)/shard_map/while/body/eval_jaxpr/psum | solution.py:156
  473.8 13.4 %collective-permute-start = (f32[1,230,256]{2,1,0:T(8,128)S(1)}, f32[1,230,256]{2,1,0:T(8,128)S(1)}, u32[]{:S(2)}, u32[]{:S(2)}) collective-permute-start(f32[1,230,256]{2,1,0:T(8,128)S(1)} %pad_maximum_fusion.2), channel_id=1, source_target_pairs={{0,8},{8,16},{16,24},{1,9},{9,17},{17,25},{2,10},{10,18},{18,26},{... | collective-permute-start | bytes 706568 | tf_op jit(solution)/shard_map/while/body/eval_jaxpr/ppermute | solution.py:14
  487.5 5.9 dynamic_update_slice.31
  503.8 24.8 %all-gather.3 = f32[8,20,256]{2,1,0:T(8,128)S(1)} all-gather(f32[1,20,256]{2,1,0:T(8,128)S(1)} %slice.5342), channel_id=2, replica_groups=mesh['section'=4,'obs'=8] {'obs'}, dimensions={0}, use_global_device_ids=true | all-gather | bytes 184320 | tf_op jit(solution)/shard_map/while/body/eval_jaxpr/all_gather | solution.py:144
  535.4 17.5 %psum.19 = f32[1,2]{1,0:T(1,128)S(1)} all-reduce(f32[1,2]{1,0:T(1,128)S(1)} %maximum_bitcast_fusion.6), channel_id=1, replica_groups=mesh['section'=4,'obs'=8] {'obs'}, use_global_device_ids=true, to_apply=%region_7.8 | all-reduce | flops 2 | bytes 16 | tf_op jit(solution)/shard_map/while/body/eval_jaxpr/psum | solution.py:156
  571.0 13.2 %collective-permute-start = (f32[1,230,256]{2,1,0:T(8,128)S(1)}, f32[1,230,256]{2,1,0:T(8,128)S(1)}, u32[]{:S(2)}, u32[]{:S(2)}) collective-permute-start(f32[1,230,256]{2,1,0:T(8,128)S(1)} %pad_maximum_fusion.2), channel_id=1, source_target_pairs={{0,8},{8,16},{16,24},{1,9},{9,17},{17,25},{2,10},{10,18},{18,26},{... | collective-permute-start | bytes 706568 | tf_op jit(solution)/shard_map/while/body/eval_jaxpr/ppermute | solution.py:14
  584.6 5.9 dynamic_update_slice.31
  600.9 24.5 %all-gather.3 = f32[8,20,256]{2,1,0:T(8,128)S(1)} all-gather(f32[1,20,256]{2,1,0:T(8,128)S(1)} %slice.5342), channel_id=2, replica_groups=mesh['section'=4,'obs'=8] {'obs'}, dimensions={0}, use_global_device_ids=true | all-gather | bytes 184320 | tf_op jit(solution)/shard_map/while/body/eval_jaxpr/all_gather | solution.py:144
  632.1 18.0 %psum.19 = f32[1,2]{1,0:T(1,128)S(1)} all-reduce(f32[1,2]{1,0:T(1,128)S(1)} %maximum_bitcast_fusion.6), channel_id=1, replica_groups=mesh['section'=4,'obs'=8] {'obs'}, use_global_device_ids=true, to_apply=%region_7.8 | all-reduce | flops 2 | bytes 16 | tf_op jit(solution)/shard_map/while/body/eval_jaxpr/psum | solution.py:156
  668.2 13.1 %collective-permute-start = (f32[1,230,256]{2,1,0:T(8,128)S(1)}, f32[1,230,256]{2,1,0:T(8,128)S(1)}, u32[]{:S(2)}, u32[]{:S(2)}) collective-permute-start(f32[1,230,256]{2,1,0:T(8,128)S(1)} %pad_maximum_fusion.2), channel_id=1, source_target_pairs={{0,8},{8,16},{16,24},{1,9},{9,17},{17,25},{2,10},{10,18},{18,26},{... | collective-permute-start | bytes 706568 | tf_op jit(solution)/shard_map/while/body/eval_jaxpr/ppermute | solution.py:14
  681.7 5.9 dynamic_update_slice.31
  (648 shorter events, 214.5 us)
Async XLA Ops:
  2.2 0.7 copy-start.4
  2.3 0.7 copy-start.5
  7.5 60.4 %all-to-all-start.1 = ((f32[1,8,8]{2,0,1:T(1,128)}), f32[1,8,8]{2,0,1:T(1,128)S(1)}, u32[]{:S(2)}, u32[]{:S(2)}) async-start(f32[1,8,8]{2,0,1:T(1,128)} %bitcast.2462), calls=%async_computation.1 | async-start | bytes 8192 | tf_op jit(solution)/shard_map/while/body/eval_jaxpr/all_to_all | solution.py:160
  68.0 9.1 %all-to-all-start = ((f32[1,8,8,230]{3,2,0,1:T(8,128)}), f32[1,8,8,230]{3,2,0,1:T(8,128)S(1)}, u32[]{:S(2)}, u32[]{:S(2)}) async-start(f32[1,8,8,230]{3,2,0,1:T(8,128)} %convolution_bitcast_fusion.4), calls=%async_computation | async-start | bytes 131072 | tf_op jit(solution)/shard_map/while/body/eval_jaxpr/all_to_all | solution.py:159
  80.7 0.7 copy-start.1
  83.2 22.0 %collective-permute-start = (f32[1,230,256]{2,1,0:T(8,128)S(1)}, f32[1,230,256]{2,1,0:T(8,128)S(1)}, u32[]{:S(2)}, u32[]{:S(2)}) collective-permute-start(f32[1,230,256]{2,1,0:T(8,128)S(1)} %pad_maximum_fusion.2), channel_id=1, source_target_pairs={{0,8},{8,16},{16,24},{1,9},{9,17},{17,25},{2,10},{10,18},{18,26},{... | collective-permute-start | bytes 706568 | tf_op jit(solution)/shard_map/while/body/eval_jaxpr/ppermute | solution.py:14
  109.8 57.8 %all-to-all-start.1 = ((f32[1,8,8]{2,0,1:T(1,128)}), f32[1,8,8]{2,0,1:T(1,128)S(1)}, u32[]{:S(2)}, u32[]{:S(2)}) async-start(f32[1,8,8]{2,0,1:T(1,128)} %bitcast.2462), calls=%async_computation.1 | async-start | bytes 8192 | tf_op jit(solution)/shard_map/while/body/eval_jaxpr/all_to_all | solution.py:160
  167.6 9.1 %all-to-all-start = ((f32[1,8,8,230]{3,2,0,1:T(8,128)}), f32[1,8,8,230]{3,2,0,1:T(8,128)S(1)}, u32[]{:S(2)}, u32[]{:S(2)}) async-start(f32[1,8,8,230]{3,2,0,1:T(8,128)} %convolution_bitcast_fusion.4), calls=%async_computation | async-start | bytes 131072 | tf_op jit(solution)/shard_map/while/body/eval_jaxpr/all_to_all | solution.py:159
  180.4 0.7 copy-start.1
  182.9 19.4 %collective-permute-start = (f32[1,230,256]{2,1,0:T(8,128)S(1)}, f32[1,230,256]{2,1,0:T(8,128)S(1)}, u32[]{:S(2)}, u32[]{:S(2)}) collective-permute-start(f32[1,230,256]{2,1,0:T(8,128)S(1)} %pad_maximum_fusion.2), channel_id=1, source_target_pairs={{0,8},{8,16},{16,24},{1,9},{9,17},{17,25},{2,10},{10,18},{18,26},{... | collective-permute-start | bytes 706568 | tf_op jit(solution)/shard_map/while/body/eval_jaxpr/ppermute | solution.py:14
  206.9 57.5 %all-to-all-start.1 = ((f32[1,8,8]{2,0,1:T(1,128)}), f32[1,8,8]{2,0,1:T(1,128)S(1)}, u32[]{:S(2)}, u32[]{:S(2)}) async-start(f32[1,8,8]{2,0,1:T(1,128)} %bitcast.2462), calls=%async_computation.1 | async-start | bytes 8192 | tf_op jit(solution)/shard_map/while/body/eval_jaxpr/all_to_all | solution.py:160
  264.4 9.1 %all-to-all-start = ((f32[1,8,8,230]{3,2,0,1:T(8,128)}), f32[1,8,8,230]{3,2,0,1:T(8,128)S(1)}, u32[]{:S(2)}, u32[]{:S(2)}) async-start(f32[1,8,8,230]{3,2,0,1:T(8,128)} %convolution_bitcast_fusion.4), calls=%async_computation | async-start | bytes 131072 | tf_op jit(solution)/shard_map/while/body/eval_jaxpr/all_to_all | solution.py:159
  277.1 0.7 copy-start.1
  279.6 19.7 %collective-permute-start = (f32[1,230,256]{2,1,0:T(8,128)S(1)}, f32[1,230,256]{2,1,0:T(8,128)S(1)}, u32[]{:S(2)}, u32[]{:S(2)}) collective-permute-start(f32[1,230,256]{2,1,0:T(8,128)S(1)} %pad_maximum_fusion.2), channel_id=1, source_target_pairs={{0,8},{8,16},{16,24},{1,9},{9,17},{17,25},{2,10},{10,18},{18,26},{... | collective-permute-start | bytes 706568 | tf_op jit(solution)/shard_map/while/body/eval_jaxpr/ppermute | solution.py:14
  303.9 57.8 %all-to-all-start.1 = ((f32[1,8,8]{2,0,1:T(1,128)}), f32[1,8,8]{2,0,1:T(1,128)S(1)}, u32[]{:S(2)}, u32[]{:S(2)}) async-start(f32[1,8,8]{2,0,1:T(1,128)} %bitcast.2462), calls=%async_computation.1 | async-start | bytes 8192 | tf_op jit(solution)/shard_map/while/body/eval_jaxpr/all_to_all | solution.py:160
  361.8 9.1 %all-to-all-start = ((f32[1,8,8,230]{3,2,0,1:T(8,128)}), f32[1,8,8,230]{3,2,0,1:T(8,128)S(1)}, u32[]{:S(2)}, u32[]{:S(2)}) async-start(f32[1,8,8,230]{3,2,0,1:T(8,128)} %convolution_bitcast_fusion.4), calls=%async_computation | async-start | bytes 131072 | tf_op jit(solution)/shard_map/while/body/eval_jaxpr/all_to_all | solution.py:159
  374.5 0.7 copy-start.1
  377.0 19.4 %collective-permute-start = (f32[1,230,256]{2,1,0:T(8,128)S(1)}, f32[1,230,256]{2,1,0:T(8,128)S(1)}, u32[]{:S(2)}, u32[]{:S(2)}) collective-permute-start(f32[1,230,256]{2,1,0:T(8,128)S(1)} %pad_maximum_fusion.2), channel_id=1, source_target_pairs={{0,8},{8,16},{16,24},{1,9},{9,17},{17,25},{2,10},{10,18},{18,26},{... | collective-permute-start | bytes 706568 | tf_op jit(solution)/shard_map/while/body/eval_jaxpr/ppermute | solution.py:14
  401.0 57.5 %all-to-all-start.1 = ((f32[1,8,8]{2,0,1:T(1,128)}), f32[1,8,8]{2,0,1:T(1,128)S(1)}, u32[]{:S(2)}, u32[]{:S(2)}) async-start(f32[1,8,8]{2,0,1:T(1,128)} %bitcast.2462), calls=%async_computation.1 | async-start | bytes 8192 | tf_op jit(solution)/shard_map/while/body/eval_jaxpr/all_to_all | solution.py:160
  458.5 9.1 %all-to-all-start = ((f32[1,8,8,230]{3,2,0,1:T(8,128)}), f32[1,8,8,230]{3,2,0,1:T(8,128)S(1)}, u32[]{:S(2)}, u32[]{:S(2)}) async-start(f32[1,8,8,230]{3,2,0,1:T(8,128)} %convolution_bitcast_fusion.4), calls=%async_computation | async-start | bytes 131072 | tf_op jit(solution)/shard_map/while/body/eval_jaxpr/all_to_all | solution.py:159
  471.3 0.7 copy-start.1
  473.8 19.7 %collective-permute-start = (f32[1,230,256]{2,1,0:T(8,128)S(1)}, f32[1,230,256]{2,1,0:T(8,128)S(1)}, u32[]{:S(2)}, u32[]{:S(2)}) collective-permute-start(f32[1,230,256]{2,1,0:T(8,128)S(1)} %pad_maximum_fusion.2), channel_id=1, source_target_pairs={{0,8},{8,16},{16,24},{1,9},{9,17},{17,25},{2,10},{10,18},{18,26},{... | collective-permute-start | bytes 706568 | tf_op jit(solution)/shard_map/while/body/eval_jaxpr/ppermute | solution.py:14
  498.1 57.7 %all-to-all-start.1 = ((f32[1,8,8]{2,0,1:T(1,128)}), f32[1,8,8]{2,0,1:T(1,128)S(1)}, u32[]{:S(2)}, u32[]{:S(2)}) async-start(f32[1,8,8]{2,0,1:T(1,128)} %bitcast.2462), calls=%async_computation.1 | async-start | bytes 8192 | tf_op jit(solution)/shard_map/while/body/eval_jaxpr/all_to_all | solution.py:160
  555.8 9.1 %all-to-all-start = ((f32[1,8,8,230]{3,2,0,1:T(8,128)}), f32[1,8,8,230]{3,2,0,1:T(8,128)S(1)}, u32[]{:S(2)}, u32[]{:S(2)}) async-start(f32[1,8,8,230]{3,2,0,1:T(8,128)} %convolution_bitcast_fusion.4), calls=%async_computation | async-start | bytes 131072 | tf_op jit(solution)/shard_map/while/body/eval_jaxpr/all_to_all | solution.py:159
  568.5 0.7 copy-start.1
  571.0 19.5 %collective-permute-start = (f32[1,230,256]{2,1,0:T(8,128)S(1)}, f32[1,230,256]{2,1,0:T(8,128)S(1)}, u32[]{:S(2)}, u32[]{:S(2)}) collective-permute-start(f32[1,230,256]{2,1,0:T(8,128)S(1)} %pad_maximum_fusion.2), channel_id=1, source_target_pairs={{0,8},{8,16},{16,24},{1,9},{9,17},{17,25},{2,10},{10,18},{18,26},{... | collective-permute-start | bytes 706568 | tf_op jit(solution)/shard_map/while/body/eval_jaxpr/ppermute | solution.py:14
  595.1 57.8 %all-to-all-start.1 = ((f32[1,8,8]{2,0,1:T(1,128)}), f32[1,8,8]{2,0,1:T(1,128)S(1)}, u32[]{:S(2)}, u32[]{:S(2)}) async-start(f32[1,8,8]{2,0,1:T(1,128)} %bitcast.2462), calls=%async_computation.1 | async-start | bytes 8192 | tf_op jit(solution)/shard_map/while/body/eval_jaxpr/all_to_all | solution.py:160
  652.9 9.1 %all-to-all-start = ((f32[1,8,8,230]{3,2,0,1:T(8,128)}), f32[1,8,8,230]{3,2,0,1:T(8,128)S(1)}, u32[]{:S(2)}, u32[]{:S(2)}) async-start(f32[1,8,8,230]{3,2,0,1:T(8,128)} %convolution_bitcast_fusion.4), calls=%async_computation | async-start | bytes 131072 | tf_op jit(solution)/shard_map/while/body/eval_jaxpr/all_to_all | solution.py:159
  665.7 0.7 copy-start.1
  668.2 19.4 %collective-permute-start = (f32[1,230,256]{2,1,0:T(8,128)S(1)}, f32[1,230,256]{2,1,0:T(8,128)S(1)}, u32[]{:S(2)}, u32[]{:S(2)}) collective-permute-start(f32[1,230,256]{2,1,0:T(8,128)S(1)} %pad_maximum_fusion.2), channel_id=1, source_target_pairs={{0,8},{8,16},{16,24},{1,9},{9,17},{17,25},{2,10},{10,18},{18,26},{... | collective-permute-start | bytes 706568 | tf_op jit(solution)/shard_map/while/body/eval_jaxpr/ppermute | solution.py:14
  687.6 0.9 copy-start.2
  687.6 0.9 copy-start.3
  (15 other events, 9.7 us)
